TPU v7x, 128 devices: a whole 4x4x4 slice. The times are simulated.
128 devices in a mesh: group: 4 (over z_lo, core), dp: 2 (over z_hi), tensor: 16 (over x, y).
Axes of the slice: x: 4, y: 4, z: 4 (z_hi: 2, z_lo: 2; z = z_hi * 2 + z_lo), core: 2. Of those that a mesh axis runs over, the one named last changes fastest.
Arguments:
- tokens: bfloat16 [2048, 8, 2048], P('tensor', ('group', 'dp')), may hold values from -6 to 6
- cotangent: bfloat16 [2048, 8, 2048], P('tensor', ('group', 'dp')), may hold values from -6 to 6
- lengths: int32 [8], replicated, may hold values from 1 to 2048, 9830 in all
- ln1_gain: float32 [2048], replicated, may hold values from 0.25 to 1.75
- ln1_bias: float32 [2048], replicated, may hold values from -1.75 to 1.75
- w_qkv: bfloat16 [2048, 3, 16, 128], P(None, None, 'tensor'), may hold values from -0.125 to 0.125
- b_qv: float32 [2, 2048], P(None, 'tensor'), may hold values from -1.75 to 1.75
- w_o: bfloat16 [16, 128, 2048], P('tensor'), may hold values from -0.75 to 0.75
- b_o: float32 [2048], replicated, may hold values from -1.75 to 1.75
- ln2_gain: float32 [2048], replicated, may hold values from 0.25 to 1.75
- ln2_bias: float32 [2048], replicated, may hold values from -1.75 to 1.75
- w_in: bfloat16 [2048, 8192], P(None, 'tensor'), may hold values from -0.125 to 0.125
- b_in: float32 [8192], P('tensor'), may hold values from -1.75 to 1.75
- w_out: bfloat16 [8192, 2048], P('tensor'), may hold values from -0.0625 to 0.0625
- b_out: float32 [2048], replicated, may hold values from -1.75 to 1.75
Outputs:
- output: bfloat16 [2048, 8, 2048], P('tensor', ('group', 'dp'))
- input_grad: bfloat16 [2048, 8, 2048], P('tensor', ('group', 'dp'))
- d_ln1_gain: float32 [2048], P(('group', 'dp', 'tensor'))
- d_ln1_bias: float32 [2048], P(('group', 'dp', 'tensor'))
- d_w_qkv: float32 [2048, 3, 16, 128], P(('group', 'dp'), None, 'tensor')
- d_b_qv: float32 [2, 2048], P(None, ('group', 'dp', 'tensor'))
- d_w_o: float32 [16, 128, 2048], P('tensor', None, ('group', 'dp'))
- d_b_o: float32 [2048], P(('group', 'dp', 'tensor'))
- d_ln2_gain: float32 [2048], P(('group', 'dp', 'tensor'))
- d_ln2_bias: float32 [2048], P(('group', 'dp', 'tensor'))
- d_w_in: float32 [2048, 8192], P(('group', 'dp'), 'tensor')
- d_b_in: float32 [8192], P(('group', 'dp', 'tensor'))
- d_w_out: float32 [8192, 2048], P('tensor', ('group', 'dp'))
- d_b_out: float32 [2048], P(('group', 'dp', 'tensor'))
Inputs may be any that keep to these rules, and one draw needn't show every extreme that they name: The true lengths of the 8 sequences sum to 9830.
All inputs are finite; a program needn't handle non-finite values.
Results may differ from a plain program's by a relative error of at most 0.02.
Values may be sent and summed in bfloat16 or wider, within the bound.
No kernel may reach another device: no remote copies, remote signals or barrier semaphores. Data moves between devices by JAX's collectives and lax.ppermute only.
A program may use at most 192 MiB of HBM per device.

v0:
```python
from functools import partial
import math
import jax
import jax.numpy as jnp
from jax import lax
from jax.sharding import PartitionSpec as P

EPS = 1e-05
NEGATIVE = -1e30


def layer_norm(value, gain, shift):
    mean = jnp.mean(value, axis=-1, keepdims=True)
    centred = value - mean
    spread = jnp.mean(centred * centred, axis=-1, keepdims=True)
    return centred * lax.rsqrt(spread + EPS) * gain + shift


def gelu_tanh(value):
    return jax.nn.gelu(value, approximate=True)


def block_scores(rows_query, key_rows, first, length, score_scale):
    count = rows_query.shape[0]
    key_pos = jnp.arange(key_rows.shape[0], dtype=jnp.int32)
    query_pos = first + jnp.arange(count, dtype=jnp.int32)
    valid = (key_pos[None, :] <= query_pos[:, None]) & (key_pos[None, :] < length)
    scores = (
        lax.dot_general(
            rows_query, key_rows, (((1,), (1,)), ((), ())), preferred_element_type=jnp.float32
        )
        * score_scale
    )
    return (jnp.where(valid, scores, NEGATIVE), valid)


def attend_forward(item, block_rows, score_scale):
    query, key_rows, value_rows, length = item
    outputs = []
    log_parts = []
    for first in range(0, query.shape[0], block_rows):
        rows_query = query[first : first + block_rows]
        scores, valid = block_scores(rows_query, key_rows, first, length, score_scale)
        peak = jnp.max(scores, axis=-1, keepdims=True)
        expo = jnp.exp(scores - peak)
        weight_sum = jnp.sum(expo, axis=-1, keepdims=True)
        probs = (expo / weight_sum).astype(jnp.bfloat16)
        outputs.append(
            jnp.dot(probs, value_rows, preferred_element_type=jnp.float32).astype(jnp.bfloat16)
        )
        log_parts.append((peak + jnp.log(weight_sum))[:, 0])
    return (jnp.concatenate(outputs, 0), jnp.concatenate(log_parts, 0))


def attend_backward(item, block_rows, score_scale):
    query, key_rows, value_rows, length, grad_out, log_sums = item
    key_grad = jnp.zeros(key_rows.shape, jnp.float32)
    value_grad = jnp.zeros(value_rows.shape, jnp.float32)
    query_parts = []
    for first in range(0, query.shape[0], block_rows):
        rows_query = query[first : first + block_rows]
        scores, valid = block_scores(rows_query, key_rows, first, length, score_scale)
        probs = jnp.where(valid, jnp.exp(scores - log_sums[first : first + block_rows, None]), 0.0)
        grad_rows = grad_out[first : first + block_rows]
        probs_grad = lax.dot_general(
            grad_rows, value_rows, (((1,), (1,)), ((), ())), preferred_element_type=jnp.float32
        )
        inner = jnp.sum(probs * probs_grad, axis=-1, keepdims=True)
        score_grad = (probs * (probs_grad - inner)).astype(jnp.bfloat16)
        query_parts.append(
            jnp.dot(score_grad, key_rows, preferred_element_type=jnp.float32) * score_scale
        )
        key_grad = (
            key_grad
            + lax.dot_general(
                score_grad, rows_query, (((0,), (0,)), ((), ())), preferred_element_type=jnp.float32
            )
            * score_scale
        )
        value_grad = value_grad + lax.dot_general(
            probs.astype(jnp.bfloat16),
            grad_rows,
            (((0,), (0,)), ((), ())),
            preferred_element_type=jnp.float32,
        )
    return (
        jnp.concatenate(query_parts, 0).astype(jnp.bfloat16),
        key_grad.astype(jnp.bfloat16),
        value_grad.astype(jnp.bfloat16),
    )


def shards(
    tokens,
    cotangent,
    lengths,
    ln1_gain,
    ln1_bias,
    w_qkv,
    b_qv,
    w_o,
    b_o,
    ln2_gain,
    ln2_bias,
    w_in,
    b_in,
    w_out,
    b_out,
):
    row_count, seq_count, model_width = tokens.shape
    tensor_count = lax.axis_size("tensor")
    tensor_rank = lax.axis_index("tensor")
    seq_total = row_count * tensor_count
    local_heads = w_qkv.shape[2]
    head_size = w_qkv.shape[3]
    local_width = local_heads * head_size
    hidden = w_in.shape[1]
    block_rows = min(512, seq_total)
    score_scale = 1.0 / math.sqrt(head_size)
    group_count = lax.axis_size("group")
    group_rank = lax.axis_index("group")
    member = group_rank * lax.axis_size("dp") + lax.axis_index("dp")
    seq_lengths = lax.dynamic_slice_in_dim(lengths, member * seq_count, seq_count, 0)
    group_totals = jnp.sum(lengths.reshape(group_count, -1), axis=1).astype(jnp.float32)
    factor = (
        group_count
        * lax.dynamic_index_in_dim(group_totals, group_rank, 0, keepdims=False)
        / jnp.sum(group_totals)
    )
    inputs = tokens.astype(jnp.float32)
    normed_low = layer_norm(inputs, ln1_gain, ln1_bias).astype(jnp.bfloat16)
    normed_full = lax.all_gather(normed_low, "tensor", axis=0, tiled=True)
    joint_weight = w_qkv.reshape(model_width, 3 * local_width)
    projected = jnp.dot(
        normed_full.reshape(seq_total * seq_count, model_width),
        joint_weight,
        preferred_element_type=jnp.float32,
    )
    projected = projected.reshape(seq_total, seq_count, 3, local_width)
    query = (projected[:, :, 0] + b_qv[0]).astype(jnp.bfloat16)
    keys = projected[:, :, 1].astype(jnp.bfloat16)
    values = (projected[:, :, 2] + b_qv[1]).astype(jnp.bfloat16)

    def per_item(array):
        shaped = array.reshape(seq_total, seq_count, local_heads, head_size)
        return jnp.transpose(shaped, (1, 2, 0, 3)).reshape(
            seq_count * local_heads, seq_total, head_size
        )

    def per_row(array):
        shaped = array.reshape(seq_count, local_heads, seq_total, head_size)
        return jnp.transpose(shaped, (2, 0, 1, 3)).reshape(seq_total, seq_count, local_width)

    query_items = per_item(query)
    key_items = per_item(keys)
    value_items = per_item(values)
    item_lengths = jnp.repeat(seq_lengths, local_heads)
    heads_out, log_sums = lax.map(
        partial(attend_forward, block_rows=block_rows, score_scale=score_scale),
        (query_items, key_items, value_items, item_lengths),
    )
    attended = per_row(heads_out)
    out_weight = w_o.reshape(local_width, model_width)
    positions = tensor_rank * row_count + jnp.arange(row_count, dtype=jnp.int32)
    live = positions[:, None] < seq_lengths[None, :]
    upstream = jnp.where(live[:, :, None], cotangent, jnp.zeros_like(cotangent))
    upstream_full = lax.all_gather(upstream, "tensor", axis=0, tiled=True)
    attention_part = jnp.einsum(
        "rse,ed->rsd", attended, out_weight, preferred_element_type=jnp.float32
    ).astype(jnp.bfloat16)
    attention_part, upstream_full = lax.optimization_barrier((attention_part, upstream_full))
    attention = (
        lax.psum_scatter(attention_part, "tensor", scatter_dimension=0, tiled=True).astype(
            jnp.float32
        )
        + b_o
    )
    middle = inputs + attention
    second_low = layer_norm(middle, ln2_gain, ln2_bias).astype(jnp.bfloat16)
    second_full = lax.all_gather(second_low, "tensor", axis=0, tiled=True)
    pre_act = (
        jnp.dot(
            second_full.reshape(seq_total * seq_count, model_width),
            w_in,
            preferred_element_type=jnp.float32,
        )
        + b_in
    )
    activated = gelu_tanh(pre_act).astype(jnp.bfloat16).reshape(seq_total, seq_count, hidden)
    feed_part = jnp.einsum(
        "rsf,fd->rsd", activated, w_out, preferred_element_type=jnp.float32
    ).astype(jnp.bfloat16)
    piece = upstream_full
    weight_grad = jnp.einsum("rsf,rsd->fd", activated, piece, preferred_element_type=jnp.float32)
    part = jnp.einsum("rsd,fd->rsf", piece, w_out, preferred_element_type=jnp.float32)
    act_grad = part
    grad_w_out = weight_grad
    gelu_back = jax.vjp(gelu_tanh, pre_act)[1]
    pre_low = gelu_back(act_grad.reshape(seq_total * seq_count, hidden))[0].astype(jnp.bfloat16)
    grad_b_in = jnp.sum(pre_low, axis=0, dtype=jnp.float32)
    grad_w_in = jnp.einsum(
        "rd,rf->df",
        second_full.reshape(seq_total * seq_count, model_width),
        pre_low,
        preferred_element_type=jnp.float32,
    )
    pre_rows = pre_low.reshape(seq_total, seq_count, hidden)
    piece = pre_rows
    second_grad = lax.psum_scatter(
        jnp.einsum("rsf,df->rsd", piece, w_in, preferred_element_type=jnp.float32).astype(
            jnp.bfloat16
        ),
        "tensor",
        scatter_dimension=0,
        tiled=True,
    ).astype(jnp.float32)
    norm_two_back = jax.vjp(layer_norm, middle, ln2_gain, ln2_bias)[1]
    middle_part, grad_ln2_gain, grad_ln2_bias = norm_two_back(second_grad)
    middle_grad = upstream.astype(jnp.float32) + middle_part
    branch_low = middle_grad.astype(jnp.bfloat16)
    grad_b_o = jnp.sum(branch_low, axis=(0, 1), dtype=jnp.float32)
    grad_b_out = jnp.sum(upstream, axis=(0, 1), dtype=jnp.float32)
    piece = lax.all_gather(branch_low, "tensor", axis=0, tiled=True)
    feed_part, piece = lax.optimization_barrier((feed_part, piece))
    feed = (
        lax.psum_scatter(feed_part, "tensor", scatter_dimension=0, tiled=True).astype(jnp.float32)
        + b_out
    )
    output = (middle + feed).astype(jnp.bfloat16)
    weight_grad = jnp.einsum("rse,rsd->ed", attended, piece, preferred_element_type=jnp.float32)
    part = jnp.einsum("rsd,ed->rse", piece, out_weight, preferred_element_type=jnp.float32)
    head_items = per_item(part.astype(jnp.bfloat16))
    grads_query, grads_keys, grads_values = lax.map(
        partial(attend_backward, block_rows=block_rows, score_scale=score_scale),
        (query_items, key_items, value_items, item_lengths, head_items, log_sums),
    )
    joint_grad = jnp.stack(
        (per_row(grads_query), per_row(grads_keys), per_row(grads_values)), axis=2
    )
    grad_b_qv = jnp.sum(joint_grad[:, :, 0::2], axis=(0, 1), dtype=jnp.float32)
    joint_rows = joint_grad.reshape(seq_total, seq_count, 3 * local_width)
    grad_w_qkv = jnp.einsum(
        "rd,rc->dc",
        normed_full.reshape(seq_total * seq_count, model_width),
        joint_rows.reshape(seq_total * seq_count, 3 * local_width),
        preferred_element_type=jnp.float32,
    )
    piece = joint_rows
    normed_grad = lax.psum_scatter(
        jnp.einsum("rsc,dc->rsd", piece, joint_weight, preferred_element_type=jnp.float32).astype(
            jnp.bfloat16
        ),
        "tensor",
        scatter_dimension=0,
        tiled=True,
    ).astype(jnp.float32)
    norm_one_back = jax.vjp(layer_norm, inputs, ln1_gain, ln1_bias)[1]
    input_part, grad_ln1_gain, grad_ln1_bias = norm_one_back(normed_grad)
    input_grad = (middle_grad + input_part).astype(jnp.bfloat16)
    summed = (
        halving_sum(grad_w_qkv.reshape(model_width, 3, local_heads, head_size) * factor, 0),
        halving_sum(weight_grad.reshape(local_heads, head_size, model_width) * factor, 2),
        halving_sum(grad_w_in * factor, 0),
        halving_sum(grad_w_out * factor, 1),
    )
    in_full = lax.dynamic_update_slice_in_dim(
        jnp.zeros((hidden * tensor_count,), jnp.float32), grad_b_in, tensor_rank * hidden, 0
    )
    joint_full = lax.dynamic_update_slice_in_dim(
        jnp.zeros((2, local_width * tensor_count), jnp.float32),
        grad_b_qv,
        tensor_rank * local_width,
        1,
    )
    shard_count = group_count * lax.axis_size("dp")
    vectors = (
        grad_ln1_gain,
        grad_ln1_bias,
        grad_b_o,
        grad_ln2_gain,
        grad_ln2_bias,
        grad_b_out,
        joint_full[0],
        joint_full[1],
        in_full,
    )
    pieces = [
        jnp.transpose((item * factor).reshape(shard_count, tensor_count, -1), (1, 0, 2))
        for item in vectors
    ]
    widths = [piece.shape[2] for piece in pieces]
    packed = jnp.concatenate(pieces, 2)
    packed = halving_steps(
        packed,
        0,
        [
            ("tensor", tensor_count, 8),
            ("tensor", tensor_count, 4),
            ("tensor", tensor_count, 2),
            ("tensor", tensor_count, 1),
        ],
    )
    packed = halving_steps(
        packed,
        1,
        [("group", group_count, 2), ("group", group_count, 1), ("dp", lax.axis_size("dp"), 1)],
    )
    flat = packed.reshape(-1)
    parts = []
    offset = 0
    for width in widths:
        parts.append(flat[offset : offset + width])
        offset += width
    return (
        output,
        input_grad,
        parts[0],
        parts[1],
        summed[0],
        jnp.stack((parts[6], parts[7])),
        summed[1],
        parts[2],
        parts[3],
        parts[4],
        summed[2],
        parts[8],
        summed[3],
        parts[5],
    )


def halving_steps(value, dim, steps, send_type=None):
    for axis, size, bit in steps:
        half = value.shape[dim] // 2
        low_half = lax.slice_in_dim(value, 0, half, axis=dim)
        high_half = lax.slice_in_dim(value, half, 2 * half, axis=dim)
        upper = lax.axis_index(axis) // bit % 2 == 1
        keep = jnp.where(upper, high_half, low_half)
        send = jnp.where(upper, low_half, high_half)
        if send_type is not None:
            send = send.astype(send_type)
        got = lax.ppermute(send, axis, [(i, i ^ bit) for i in range(size)])
        value = keep + got.astype(keep.dtype)
    return value


def halving_sum(value, dim):
    shape = value.shape
    groups = lax.axis_size("group")
    dps = lax.axis_size("dp")
    split = shape[:dim] + (groups * dps, shape[dim] // (groups * dps)) + shape[dim + 1 :]
    value = value.reshape(split)
    value = halving_steps(
        value, dim, [("group", groups, 2), ("group", groups, 1), ("dp", dps, 1)], jnp.bfloat16
    )
    return value.reshape(shape[:dim] + (shape[dim] // (groups * dps),) + shape[dim + 1 :])


def solution(mesh):
    in_specs = (
        P("tensor", ("group", "dp"), None),
        P("tensor", ("group", "dp"), None),
        P(),
        P(),
        P(),
        P(None, None, "tensor", None),
        P(None, "tensor"),
        P("tensor", None, None),
        P(),
        P(),
        P(),
        P(None, "tensor"),
        P("tensor"),
        P("tensor", None),
        P(),
    )
    out_specs = (
        P("tensor", ("group", "dp"), None),
        P("tensor", ("group", "dp"), None),
        P(("group", "dp", "tensor")),
        P(("group", "dp", "tensor")),
        P(("group", "dp"), None, "tensor", None),
        P(None, ("group", "dp", "tensor")),
        P("tensor", None, ("group", "dp")),
        P(("group", "dp", "tensor")),
        P(("group", "dp", "tensor")),
        P(("group", "dp", "tensor")),
        P(("group", "dp"), "tensor"),
        P(("group", "dp", "tensor")),
        P("tensor", ("group", "dp")),
        P(("group", "dp", "tensor")),
    )
    return jax.shard_map(shards, mesh=mesh, in_specs=in_specs, out_specs=out_specs, check_vma=False)
```

profile of v0, /device:TPU:0, one launch (start us, length us, event | category | flops | bytes accessed | tf_op | source)
XLA Modules:
  0.0 779.4 jit_solution(8731599573753859071)
XLA Ops:
  20.3 65.2 %all-gather.5.cloned.1.call-done = bf16[2048,1,2048]{2,0,1:T(8,128)(2,1)} async-done(((bf16[128,1,2048]{2,0,1:T(8,128)(2,1)}), bf16[2048,1,2048]{2,0,1:T(8,128)(2,1)}) %all-gather.5.cloned.1.call-update) | async-done | bytes 8388624 | tf_op jit(solution)/shard_map/all_gather | solution.py:132
  85.5 7.4 fusion.33
  98.0 4.2 online-softmax.3
  103.2 5.2 fusion.126
  113.4 5.2 fusion.125
  123.6 4.8 fusion.124
  128.4 4.4 online-softmax
  133.8 5.6 convert_bitcast_fusion.3
  139.4 19.1 %all-gather.7.cloned.1.call-done = bf16[2048,1,2048]{2,0,1:T(8,128)(2,1)} async-done(((bf16[128,1,2048]{2,0,1:T(8,128)(2,1)}), bf16[2048,1,2048]{2,0,1:T(8,128)(2,1)}) %all-gather.7.cloned.1.call-update) | async-done | bytes 8388624 | tf_op jit(solution)/shard_map/all_gather | solution.py:167
  158.6 88.1 %reduce-scatter.5.cloned.1.call-done = bf16[128,1,2048]{2,0,1:T(8,128)(2,1)} async-done(((bf16[2048,1,2048]{2,0,1:T(8,128)(2,1)}), bf16[128,1,2048]{2,0,1:T(8,128)(2,1)}) %reduce-scatter.5.cloned.1.call-update) | async-done | bytes 524304 | tf_op jit(solution)/shard_map/reduce_scatter | solution.py:173
  251.7 70.2 %all-gather.9.cloned.1.call-done = bf16[2048,1,2048]{2,0,1:T(8,128)(2,1)} async-done(((bf16[128,1,2048]{2,0,1:T(8,128)(2,1)}), bf16[2048,1,2048]{2,0,1:T(8,128)(2,1)}) %all-gather.9.cloned.1.call-update) | async-done | bytes 8388624 | tf_op jit(solution)/shard_map/all_gather | solution.py:180
  321.9 7.5 fusion.10
  329.4 13.1 %convert_reduce_fusion = (f32[512]{0:T(512)}, bf16[2048,512]{1,0:T(8,128)(2,1)S(1)}) fusion(f32[2048,512]{1,0:T(8,128)S(1)} %fusion.10, f32[512]{0:T(512)S(1)} %copy-done.85, bf16[512,2048]{1,0:T(8,128)(2,1)S(1)} %copy-done, bf16[2048,1,2048]{2,0,1:T(8,128)(2,1)} %all-gather.7.cloned.1.call-done), kind=kOutput, calls=%fused_computation.29 | convolution fusion | flops 4319084032 | bytes 16781312 | tf_op jit(solution)/shard_map/rsd,fd->rsf/dot_general | solution.py:195
  343.9 6.9 convert_bitcast_fusion.1
  350.9 84.8 %reduce-scatter.7.cloned.1.call-done = bf16[128,1,2048]{2,0,1:T(8,128)(2,1)} async-done(((bf16[2048,1,2048]{2,0,1:T(8,128)(2,1)}), bf16[128,1,2048]{2,0,1:T(8,128)(2,1)}) %reduce-scatter.7.cloned.1.call-update) | async-done | bytes 524304 | tf_op jit(solution)/shard_map/reduce_scatter | solution.py:209
  450.4 15.8 %convert_bitcast_fusion.2 = bf16[2048,1,2048]{2,0,1:T(8,128)(2,1)} fusion(bf16[512,2048]{1,0:T(8,128)(2,1)S(1)} %copy-done, f32[2048,512]{1,0:T(8,128)S(1)} %copy-done.89, f32[512]{0:T(512)S(1)} %copy-done.85), kind=kOutput, calls=%fused_computation.18 | convolution fusion | flops 4309647360 | bytes 14682112 | tf_op jit(solution)/shard_map/rsf,fd->rsd/dot_general | solution.py:190
  466.2 45.6 %all-gather.11.cloned.1.call-done = bf16[2048,1,2048]{2,0,1:T(8,128)(2,1)} async-done(((bf16[128,1,2048]{2,0,1:T(8,128)(2,1)}), bf16[2048,1,2048]{2,0,1:T(8,128)(2,1)}) %all-gather.11.cloned.1.call-update) | async-done | bytes 8388624 | tf_op jit(solution)/shard_map/all_gather | solution.py:223
  511.8 5.8 fusion.45
  530.8 10.9 %multiply_reduce_fusion = (f32[512]{0:T(512)}, f32[512]{0:T(512)}, f32[512]{0:T(512)}, f32[512]{0:T(512)}, f32[512,2048]{1,0:T(8,128)}) fusion(f32[512,2048]{1,0:T(8,128)S(1)} %copy-done.2, f32[512]{0:T(512)S(1)} %copy-done.59, pred[2048]{0:T(1024)(128)(4,1)S(1)} %iota_compare_fusion.4, s32[512]{0:T(512)S(1)} %copy-done.52, f32[512,2048]{1,0:T(8,128)} %fusion.108, ...), kind=kOutput, calls=%fused_computation.31 | convolution fusion | flops 293599232 | bytes 34234368 | tf_op jit(solution)/shard_map/while/body/eval_jaxpr/dot_general | solution.py:65
  541.7 9.5 %multiply_convert_fusion = (bf16[512,2048]{1,0:T(8,128)(2,1)S(1)}, bf16[512,2048]{1,0:T(8,128)(2,1)}, bf16[512,2048]{1,0:T(8,128)(2,1)S(1)}) fusion(f32[512,2048]{1,0:T(8,128)} %get-tuple-element.119, f32[512]{0:T(512)} %get-tuple-element.82, f32[512,2048]{1,0:T(8,128)S(1)} %copy-done.2, f32[512]{0:T(512)} %get-tuple-element.124, ...), kind=kLoop, calls=%fused_computation.30 | loop fusion | flops 22020096 | bytes 31475712 | tf_op jit(solution)/shard_map/while/body/eval_jaxpr/convert_element_type | solution.py:69
  569.4 9.7 %convert_bitcast_fusion = bf16[2048,1,2048]{2,0,1:T(8,128)(2,1)} fusion(bf16[2048,384]{0,1:T(8,128)(2,1)} %bitcast.201, bf16[2048,384]{0,1:T(8,128)(2,1)} %bitcast.202), kind=kOutput, calls=%fused_computation.16 | convolution fusion | flops 3225419776 | bytes 11534336 | tf_op jit(solution)/shard_map/rsc,dc->rsd/dot_general | solution.py:250
  582.5 8.5 %fusion.27 = f32[512,2048]{1,0:T(8,128)S(1)} fusion(bf16[2048,1,2048]{2,0,1:T(8,128)(2,1)} %all-gather.7.cloned.1.call-done, f32[]{:T(128)S(6)} %div.167, f32[2048,512]{1,0:T(8,128)} %copy-done.88, f32[512]{0:T(512)S(1)} %copy-done.86), kind=kOutput, calls=%fused_computation.59 | convolution fusion | flops 4306501632 | bytes 16779268 | tf_op jit(solution)/shard_map/rsf,rsd->fd/dot_general | solution.py:194
  596.6 7.1 fusion.30
  614.4 17.2 %collective-permute-done.13 = bf16[4,256,512]{2,1,0:T(8,128)(2,1)} collective-permute-done((bf16[4,256,512]{2,1,0:T(8,128)(2,1)}, bf16[4,256,512]{2,1,0:T(8,128)(2,1)}, u32[]{:S(2)}, u32[]{:S(2)}) %collective-permute-start.13) | collective-permute-done | bytes 1048608 | tf_op jit(solution)/shard_map/ppermute | solution.py:342
  633.4 19.6 %collective-permute-done.16 = bf16[512,4,256]{2,0,1:T(8,128)(2,1)} collective-permute-done((bf16[512,4,256]{2,0,1:T(8,128)(2,1)}, bf16[512,4,256]{2,0,1:T(8,128)(2,1)}, u32[]{:S(2)}, u32[]{:S(2)}) %collective-permute-start.16) | collective-permute-done | bytes 1048608 | tf_op jit(solution)/shard_map/ppermute | solution.py:342
  661.9 5.2 collective-permute-done.15
  668.0 4.4 collective-permute-done.18
  676.4 4.7 fusion.42
  683.5 7.0 fusion.36
  709.7 26.8 %collective-permute-done.7 = bf16[4,256,3,1,128]{4,3,2,1,0:T(2,128)(2,1)} collective-permute-done((bf16[4,256,3,1,128]{4,3,2,1,0:T(2,128)(2,1)S(1)}, bf16[4,256,3,1,128]{4,3,2,1,0:T(2,128)(2,1)}, u32[]{:S(2)}, u32[]{:S(2)}) %collective-permute-start.7) | collective-permute-done | bytes 786464 | tf_op jit(solution)/shard_map/ppermute | solution.py:342
  736.5 4.7 copy_add_fusion
  755.1 7.4 collective-permute-done.9
  (371 shorter events, 160.5 us)
Async XLA Ops:
  7.2 322.2 %copy-start = (bf16[512,2048]{1,0:T(8,128)(2,1)S(1)}, bf16[512,2048]{1,0:T(8,128)(2,1)}, u32[]{:S(2)}) copy-start(bf16[512,2048]{1,0:T(8,128)(2,1)} %param.28) | copy-start | bytes 6291460
  7.2 78.3 %all-gather.5.cloned.1.call-start = ((), (), s32[]{:S(2)}) async-start(), calls=%async_computation.4 | async-start | bytes 8912896 | tf_op jit(solution)/shard_map/all_gather | solution.py:132
  12.2 146.3 %all-gather.7.cloned.1.call-start = ((), (), s32[]{:S(2)}) async-start(), calls=%async_computation.5 | async-start | bytes 8912896 | tf_op jit(solution)/shard_map/all_gather | solution.py:167
  16.8 229.8 %reduce-scatter.5.cloned.1.call-start = ((), (), s32[]{:S(2)}) async-start(), calls=%async_computation.6 | async-start | bytes 8912896 | tf_op jit(solution)/shard_map/reduce_scatter | solution.py:173
  139.4 107.3 %copy-start.9 = (bf16[128,1,2048]{2,0,1:T(8,128)(2,1)S(1)}, bf16[128,1,2048]{2,0,1:T(8,128)(2,1)}, u32[]{:S(2)}) copy-start(bf16[128,1,2048]{2,0,1:T(8,128)(2,1)} %param.15) | copy-start | bytes 1572868
  139.4 107.3 %copy-start.39 = (f32[2048]{0:T(1024)S(1)}, f32[2048]{0:T(1024)}, u32[]{:S(2)}) copy-start(f32[2048]{0:T(1024)} %param.23) | copy-start | bytes 24580
  139.4 110.0 %copy-start.47 = (f32[2048]{0:T(1024)S(1)}, f32[2048]{0:T(1024)}, u32[]{:S(2)}) copy-start(f32[2048]{0:T(1024)} %param.24) | copy-start | bytes 24580
  139.4 110.0 %copy-start.70 = (f32[2048]{0:T(1024)S(1)}, f32[2048]{0:T(1024)}, u32[]{:S(2)}) copy-start(f32[2048]{0:T(1024)} %param.25) | copy-start | bytes 24580
  158.6 163.3 %all-gather.9.cloned.1.call-start = ((), (), s32[]{:S(2)}) async-start(), calls=%async_computation.7 | async-start | bytes 8912896 | tf_op jit(solution)/shard_map/all_gather | solution.py:180
  251.6 184.1 %reduce-scatter.7.cloned.1.call-start = ((), (), s32[]{:S(2)}) async-start(), calls=%async_computation.8 | async-start | bytes 8912896 | tf_op jit(solution)/shard_map/reduce_scatter | solution.py:209
  350.9 160.9 %all-gather.11.cloned.1.call-start = ((), (), s32[]{:S(2)}) async-start(), calls=%async_computation.9 | async-start | bytes 8912896 | tf_op jit(solution)/shard_map/all_gather | solution.py:223
  441.6 260.6 %reduce-scatter.11.cloned.1.call-start = ((), (), s32[]{:S(2)}) async-start(), calls=%async_computation.11 | async-start | bytes 8912896 | tf_op jit(solution)/shard_map/reduce_scatter | solution.py:249
  579.1 186.7 %reduce-scatter.9.cloned.1.call-start = ((), (), s32[]{:S(2)}) async-start(), calls=%async_computation.10 | async-start | bytes 8912896 | tf_op jit(solution)/shard_map/reduce_scatter | solution.py:226
  605.1 26.5 %collective-permute-start.13 = (bf16[4,256,512]{2,1,0:T(8,128)(2,1)}, bf16[4,256,512]{2,1,0:T(8,128)(2,1)}, u32[]{:S(2)}, u32[]{:S(2)}) collective-permute-start(bf16[4,256,512]{2,1,0:T(8,128)(2,1)} %bitcast.57), channel_id=1, source_target_pairs={{0,64},{32,96},{64,0},{96,32},{1,65},{33,97},{65,1},{97,33},{2,66}... | collective-permute-start | bytes 3145736 | tf_op jit(solution)/shard_map/ppermute | solution.py:342
  610.4 42.5 %collective-permute-start.16 = (bf16[512,4,256]{2,0,1:T(8,128)(2,1)}, bf16[512,4,256]{2,0,1:T(8,128)(2,1)}, u32[]{:S(2)}, u32[]{:S(2)}) collective-permute-start(bf16[512,4,256]{2,0,1:T(8,128)(2,1)} %select_convert_fusion), channel_id=1, source_target_pairs={{0,64},{32,96},{64,0},{96,32},{1,65},{33,97},{65,1},{97,33},{2,66}... | collective-permute-start | bytes 3145736 | tf_op jit(solution)/shard_map/ppermute | solution.py:342
  633.3 21.9 %collective-permute-start.14 = (bf16[2,256,512]{2,1,0:T(8,128)(2,1)S(1)}, bf16[2,256,512]{2,1,0:T(8,128)(2,1)S(1)}, u32[]{:S(2)}, u32[]{:S(2)}) collective-permute-start(bf16[2,256,512]{2,1,0:T(8,128)(2,1)S(1)} %select_convert_fusion.4), channel_id=1, source_target_pairs={{0,32},{32,0},{64,96},{96,64},{1,33},{33,1},{65,97},{97,65},{2,34}... | collective-permute-start | bytes 1572872 | tf_op jit(solution)/shard_map/ppermute | solution.py:342
  655.0 4.4 collective-permute-start.17
  656.2 10.9 %collective-permute-start.15 = (bf16[1,256,512]{2,1,0:T(8,128)(2,1)}, bf16[1,256,512]{2,1,0:T(8,128)(2,1)S(1)}, u32[]{:S(2)}, u32[]{:S(2)}) collective-permute-start(bf16[1,256,512]{2,1,0:T(8,128)(2,1)} %select_convert_fusion.6), channel_id=1, source_target_pairs={{0,16},{16,0},{1,17},{17,1},{2,18},{18,2},{3,19},{19,3},{4,20},{20... | collective-permute-start | bytes 786440 | tf_op jit(solution)/shard_map/ppermute | solution.py:342
  660.4 12.0 %collective-permute-start.18 = (bf16[512,1,256]{2,0,1:T(8,128)(2,1)}, bf16[512,1,256]{2,0,1:T(8,128)(2,1)}, u32[]{:S(2)}, u32[]{:S(2)}) collective-permute-start(bf16[512,1,256]{2,0,1:T(8,128)(2,1)} %select_convert_fusion.5), channel_id=1, source_target_pairs={{0,16},{16,0},{1,17},{17,1},{2,18},{18,2},{3,19},{19,3},{4,20},{20... | collective-permute-start | bytes 786440 | tf_op jit(solution)/shard_map/ppermute | solution.py:342
  681.8 10.1 %collective-permute-start.10 = (bf16[1,128,4,256]{3,1,2,0:T(8,128)(2,1)S(1)}, bf16[1,128,4,256]{3,1,2,0:T(8,128)(2,1)S(1)}, u32[]{:S(2)}, u32[]{:S(2)}) collective-permute-start(bf16[1,128,4,256]{3,1,2,0:T(8,128)(2,1)S(1)} %select_convert_fusion.7), channel_id=1, source_target_pairs={{0,64},{32,96},{64,0},{96,32},{1,65},{33,97},{65,1},{97,33},{2,66}... | collective-permute-start | bytes 786440 | tf_op jit(solution)/shard_map/ppermute | solution.py:342
  692.2 1.4 collective-permute-start.11
  694.4 6.3 collective-permute-start.12
  700.2 36.4 %collective-permute-start.7 = (bf16[4,256,3,1,128]{4,3,2,1,0:T(2,128)(2,1)S(1)}, bf16[4,256,3,1,128]{4,3,2,1,0:T(2,128)(2,1)}, u32[]{:S(2)}, u32[]{:S(2)}) collective-permute-start(bf16[4,256,3,1,128]{4,3,2,1,0:T(2,128)(2,1)S(1)} %copy.55), channel_id=1, source_target_pairs={{0,64},{32,96},{64,0},{96,32},{1,65},{33,97},{65,1},{97,33},{2,66}... | collective-permute-start | bytes 2359304 | tf_op jit(solution)/shard_map/ppermute | solution.py:342
  706.6 34.6 %collective-permute-start = (f32[8,8,192]{2,0,1:T(8,128)S(1)}, f32[8,8,192]{2,0,1:T(8,128)S(1)}, u32[]{:S(2)}, u32[]{:S(2)}) collective-permute-start(f32[8,8,192]{2,0,1:T(8,128)S(1)} %slice_select_fusion.2), channel_id=1, source_target_pairs={{0,8},{1,9},{2,10},{3,11},{4,12},{5,13},{6,14},{7,15},{8,0},{9,1},... | collective-permute-start | bytes 147464 | tf_op jit(solution)/shard_map/ppermute | solution.py:342
  741.3 4.5 collective-permute-start.1
  743.6 5.4 collective-permute-start.8
  745.9 5.4 collective-permute-start.2
  751.3 3.7 collective-permute-start.3
  753.2 9.4 %collective-permute-start.9 = (bf16[1,256,3,1,128]{4,3,2,1,0:T(2,128)(2,1)S(1)}, bf16[1,256,3,1,128]{4,3,2,1,0:T(2,128)(2,1)S(1)}, u32[]{:S(2)}, u32[]{:S(2)}) collective-permute-start(bf16[1,256,3,1,128]{4,3,2,1,0:T(2,128)(2,1)S(1)} %fusion.96), channel_id=1, source_target_pairs={{0,16},{16,0},{1,17},{17,1},{2,18},{18,2},{3,19},{19,3},{4,20},{20... | collective-permute-start | bytes 589832 | tf_op jit(solution)/shard_map/ppermute | solution.py:342
  755.1 9.0 %collective-permute-start.4 = (f32[1,4,192]{2,0,1:T(1,128)S(1)}, f32[1,4,192]{2,0,1:T(1,128)S(1)}, u32[]{:S(2)}, u32[]{:S(2)}) collective-permute-start(f32[1,4,192]{2,0,1:T(1,128)S(1)} %broadcast_select_fusion.8), channel_id=1, source_target_pairs={{0,64},{32,96},{64,0},{96,32},{1,65},{33,97},{65,1},{97,33},{2,66}... | collective-permute-start | bytes 9224 | tf_op jit(solution)/shard_map/ppermute | solution.py:342
  764.0 1.2 collective-permute-start.5
  765.3 5.2 collective-permute-start.6
  (87 other events, 1435.8 us)
Sparse Core Ops, SparseCore 0:
  12.4 73.0 all-gather.4
  88.2 70.3 all-gather.6
  162.0 84.6 reduce-scatter.4
  251.8 70.0 all-gather.8
  351.0 84.6 reduce-scatter.6
  441.7 70.0 all-gather.10
  579.2 84.8 reduce-scatter.10
  667.6 85.7 reduce-scatter.8
where the time goes:
time: 789 us; the launch traced here: 779 us
  waiting for transfers between devices  461 us (58%)
  matrix products  155 us (20%)
  other arithmetic  78.1 us (10%)
  local copies, waits for them, and re-layouts  28.2 us (4%)
  starting transfers between devices  22.8 us (3%)
  between operations  17.3 us (2%)
  Pallas kernels  16.6 us (2%)
    ppermute x19, waiting for transfers between devices, halving_steps(): got = lax.ppermute(send, axis, [(i, i ^ bit) for i in range(size)])  88.2 us
    reduce_scatter x1, waiting for transfers between devices, shards(): lax.psum_scatter(attention_part, 'tensor', scatter_dimension=0, tiled=True)  88.1 us
    reduce_scatter x1, waiting for transfers between devices, shards(): lax.psum_scatter(jnp.einsum('rsf,df->rsd', piece, w_in, preferred_element...  84.8 us
    all_gather x1, waiting for transfers between devices, shards(): second_full = lax.all_gather(second_low, 'tensor', axis=0, tiled=True)  70.2 us
    all_gather x1, waiting for transfers between devices, shards(): normed_full = lax.all_gather(normed_low, 'tensor', axis=0, tiled=True)  65.2 us
    all_gather x1, waiting for transfers between devices, shards(): piece = lax.all_gather(branch_low, 'tensor', axis=0, tiled=True)  45.6 us
    ppermute x19, starting transfers between devices, halving_steps(): got = lax.ppermute(send, axis, [(i, i ^ bit) for i in range(size)])  22.5 us
    dot_general x4, matrix products, attend_backward(): lax.dot_general(grad_rows, value_rows, (((1,), (1,)), ((), ())), preferre...  21.5 us
  transfers between devices with their start and end apart: 27, of which 19 were waited for; matrix products, arithmetic and copies ran while one was open for 18% of the time, Pallas kernels for 2%

commit v1 on v0

--- a/solution.py
+++ b/solution.py
@@ -7,6 +7,28 @@
 
 EPS = 1e-05
 NEGATIVE = -1e30
+
+
+def in_order(blocks, dim):
+    lengths = list(blocks.shape[1:])
+    lengths[dim] *= blocks.shape[0]
+    return jnp.moveaxis(blocks, 0, dim).reshape(lengths)
+
+
+def collect(value, axis, dim):
+    devices = lax.axis_size(axis)
+    pairs = [(i, (i + 1) % devices) for i in range(devices)]
+    back = [(b, a) for a, b in pairs]
+    lower, upper = ([], [])
+    for turn in range(devices - 1):
+        if turn % 2 == 0:
+            lower.append(lax.ppermute(lower[-1] if lower else value, axis, pairs))
+        else:
+            upper.append(lax.ppermute(upper[-1] if upper else value, axis, back))
+    blocks = jnp.stack([*lower[::-1], value, *upper])
+    shift = lax.axis_index(axis) - len(lower)
+    blocks = blocks[(jnp.arange(devices) - shift) % devices]
+    return in_order(blocks, dim)
 
 
 def layer_norm(value, gain, shift):
@@ -220,7 +242,7 @@
     branch_low = middle_grad.astype(jnp.bfloat16)
     grad_b_o = jnp.sum(branch_low, axis=(0, 1), dtype=jnp.float32)
     grad_b_out = jnp.sum(upstream, axis=(0, 1), dtype=jnp.float32)
-    piece = lax.all_gather(branch_low, "tensor", axis=0, tiled=True)
+    piece = collect(branch_low, "tensor", 0)
     feed_part, piece = lax.optimization_barrier((feed_part, piece))
     feed = (
         lax.psum_scatter(feed_part, "tensor", scatter_dimension=0, tiled=True).astype(jnp.float32)

time: 789 us -> 843 us (1.068)
  local copies, waits for them, and re-layouts: 28.2 us -> 64.3 us
  starting transfers between devices: 22.8 us -> 55.8 us
  matrix products: 155 us -> 142 us
    ppermute x0 -> x15, waiting for transfers between devices: none -> 55.2 us  [the longest x8 53.4 us: collect(): lower.append(lax.ppermute(lower[-1] if lower else value, axis, pairs))]
    all_gather x1 -> x0, waiting for transfers between devices: 45.6 us -> none  [shards(): piece = lax.all_gather(branch_low, 'tensor', axis=0, tiled=True)]
    ppermute x0 -> x15, starting transfers between devices: none -> 40.2 us  [the longest x7 38.8 us: collect(): upper.append(lax.ppermute(upper[-1] if upper else value, axis, back))]
    unnamed x187 -> x226, local copies, waits for them, and re-layouts: 15.3 us -> 38.6 us
    ppermute x19, waiting for transfers between devices: 88.2 us -> 75.6 us  [halving_steps(): got = lax.ppermute(send, axis, [(i, i ^ bit) for i in range(size)])]
    dot_general x1, matrix products: 15.8 us -> 7.23 us  [shards(): jnp.einsum('rsf,fd->rsd', activated, w_out, preferred_element_type=jnp.fl...]
  transfers between devices with their start and end apart: 27 -> 41, of which waited for: 19 -> 27; matrix products, arithmetic and copies ran while one was open for 18% -> 20% of each run, Pallas kernels for 2% -> 2%
where the time goes in v1:
time: 843 us; the launch traced here: 833 us
  waiting for transfers between devices  458 us (54%)
  matrix products  142 us (17%)
  other arithmetic  78.7 us (9%)
  local copies, waits for them, and re-layouts  64.3 us (8%)
  starting transfers between devices  55.8 us (7%)
  between operations  17.5 us (2%)
  Pallas kernels  16.5 us (2%)
    reduce_scatter x1, waiting for transfers between devices, shards(): lax.psum_scatter(attention_part, 'tensor', scatter_dimension=0, tiled=True)  88.1 us
    reduce_scatter x1, waiting for transfers between devices, shards(): lax.psum_scatter(jnp.einsum('rsf,df->rsd', piece, w_in, preferred_element...  84.2 us
    ppermute x19, waiting for transfers between devices, halving_steps(): got = lax.ppermute(send, axis, [(i, i ^ bit) for i in range(size)])  75.6 us
    all_gather x1, waiting for transfers between devices, shards(): second_full = lax.all_gather(second_low, 'tensor', axis=0, tiled=True)  70.2 us
    all_gather x1, waiting for transfers between devices, shards(): normed_full = lax.all_gather(normed_low, 'tensor', axis=0, tiled=True)  65.2 us
    ppermute x8, waiting for transfers between devices, collect(): lower.append(lax.ppermute(lower[-1] if lower else value, axis, pairs))  53.4 us
    ppermute x7, starting transfers between devices, collect(): upper.append(lax.ppermute(upper[-1] if upper else value, axis, back))  38.8 us
    unnamed x226, local copies, waits for them, and re-layouts  38.6 us
  transfers between devices with their start and end apart: 41, of which 27 were waited for; matrix products, arithmetic and copies ran while one was open for 20% of the time, Pallas kernels for 2%

profile of v1, /device:TPU:0, one launch (start us, length us, event | category | flops | bytes accessed | tf_op | source)
XLA Modules:
  0.0 832.6 jit_solution(3685792049873574825)
XLA Ops:
  20.3 65.2 %all-gather.4.cloned.1.call-done = bf16[2048,1,2048]{2,0,1:T(8,128)(2,1)} async-done(((bf16[128,1,2048]{2,0,1:T(8,128)(2,1)}), bf16[2048,1,2048]{2,0,1:T(8,128)(2,1)}) %all-gather.4.cloned.1.call-update) | async-done | bytes 8388624 | tf_op jit(solution)/shard_map/all_gather | solution.py:154
  85.5 7.4 fusion.33
  133.8 5.6 convert_bitcast_fusion.3
  139.5 19.1 %all-gather.6.cloned.1.call-done = bf16[2048,1,2048]{2,0,1:T(8,128)(2,1)} async-done(((bf16[128,1,2048]{2,0,1:T(8,128)(2,1)}), bf16[2048,1,2048]{2,0,1:T(8,128)(2,1)}) %all-gather.6.cloned.1.call-update) | async-done | bytes 8388624 | tf_op jit(solution)/shard_map/all_gather | solution.py:189
  158.6 88.1 %reduce-scatter.5.cloned.1.call-done = bf16[128,1,2048]{2,0,1:T(8,128)(2,1)} async-done(((bf16[2048,1,2048]{2,0,1:T(8,128)(2,1)}), bf16[128,1,2048]{2,0,1:T(8,128)(2,1)}) %reduce-scatter.5.cloned.1.call-update) | async-done | bytes 524304 | tf_op jit(solution)/shard_map/reduce_scatter | solution.py:195
  251.7 70.2 %all-gather.8.cloned.1.call-done = bf16[2048,1,2048]{2,0,1:T(8,128)(2,1)} async-done(((bf16[128,1,2048]{2,0,1:T(8,128)(2,1)}), bf16[2048,1,2048]{2,0,1:T(8,128)(2,1)}) %all-gather.8.cloned.1.call-update) | async-done | bytes 8388624 | tf_op jit(solution)/shard_map/all_gather | solution.py:202
  321.9 7.6 fusion.10
  329.5 13.1 %convert_reduce_fusion = (f32[512]{0:T(512)}, bf16[2048,512]{1,0:T(8,128)(2,1)S(1)}) fusion(f32[2048,512]{1,0:T(8,128)S(1)} %fusion.10, f32[512]{0:T(512)S(1)} %copy-done.98, bf16[512,2048]{1,0:T(8,128)(2,1)S(1)} %copy-done, bf16[2048,1,2048]{2,0,1:T(8,128)(2,1)} %all-gather.6.cloned.1.call-done), kind=kOutput, calls=%fused_computation.30 | convolution fusion | flops 4319084032 | bytes 16781312 | tf_op jit(solution)/shard_map/rsd,fd->rsf/dot_general | solution.py:217
  343.9 7.0 convert_bitcast_fusion.1
  351.4 84.2 %reduce-scatter.7.cloned.1.call-done = bf16[128,1,2048]{2,0,1:T(8,128)(2,1)} async-done(((bf16[2048,1,2048]{2,0,1:T(8,128)(2,1)}), bf16[128,1,2048]{2,0,1:T(8,128)(2,1)}) %reduce-scatter.7.cloned.1.call-update) | async-done | bytes 524304 | tf_op jit(solution)/shard_map/reduce_scatter | solution.py:231
  442.1 14.3 %collective-permute-done = bf16[128,1,2048]{2,0,1:T(8,128)(2,1)S(1)} collective-permute-done((bf16[128,1,2048]{2,0,1:T(8,128)(2,1)S(1)}, bf16[128,1,2048]{2,0,1:T(8,128)(2,1)S(1)}, u32[]{:S(2)}, u32[]{:S(2)}) %collective-permute-start) | collective-permute-done | bytes 524320 | tf_op jit(solution)/shard_map/ppermute | solution.py:25
  461.8 9.4 %collective-permute-done.1 = bf16[128,1,2048]{2,0,1:T(8,128)(2,1)S(1)} collective-permute-done((bf16[128,1,2048]{2,0,1:T(8,128)(2,1)S(1)}, bf16[128,1,2048]{2,0,1:T(8,128)(2,1)S(1)}, u32[]{:S(2)}, u32[]{:S(2)}) %collective-permute-start.1) | collective-permute-done | bytes 524320 | tf_op jit(solution)/shard_map/ppermute | solution.py:25
  476.6 8.6 %collective-permute-done.2 = bf16[128,1,2048]{2,0,1:T(8,128)(2,1)} collective-permute-done((bf16[128,1,2048]{2,0,1:T(8,128)(2,1)S(1)}, bf16[128,1,2048]{2,0,1:T(8,128)(2,1)}, u32[]{:S(2)}, u32[]{:S(2)}) %collective-permute-start.2) | collective-permute-done | bytes 524320 | tf_op jit(solution)/shard_map/ppermute | solution.py:25
  485.3 5.4 collective-permute-start.10
  490.7 7.8 collective-permute-done.3
  502.3 5.4 collective-permute-start.11
  515.2 5.8 collective-permute-start.12
  529.1 5.9 collective-permute-start.13
  540.1 7.2 convert_bitcast_fusion.2
  547.3 5.6 collective-permute-start.14
  577.1 8.3 gather_fusion
  585.4 5.9 fusion.45
  600.4 10.1 %multiply_reduce_fusion = (f32[512]{0:T(512)}, f32[512]{0:T(512)}, f32[512]{0:T(512)}, f32[512]{0:T(512)}, f32[512,2048]{1,0:T(8,128)}) fusion(f32[512,2048]{1,0:T(8,128)S(1)} %copy-done.4, f32[512]{0:T(512)S(1)} %copy-done.71, pred[2048]{0:T(1024)(128)(4,1)S(1)} %iota_compare_fusion.4, s32[512]{0:T(512)S(1)} %iota_add_fusion, f32[512,2048]{1,0:T(8,128)} %fusion.108, ...), kind=kOutput, calls=%fused_computation.32 | convolution fusion | flops 293599232 | bytes 34234368 | tf_op jit(solution)/shard_map/while/body/eval_jaxpr/dot_general | solution.py:87
  610.4 9.1 %multiply_convert_fusion = (bf16[512,2048]{1,0:T(8,128)(2,1)S(1)}, bf16[512,2048]{1,0:T(8,128)(2,1)}, bf16[512,2048]{1,0:T(8,128)(2,1)S(1)}) fusion(f32[512,2048]{1,0:T(8,128)} %get-tuple-element.119, f32[512]{0:T(512)} %get-tuple-element.82, f32[512,2048]{1,0:T(8,128)S(1)} %copy-done.4, f32[512]{0:T(512)} %get-tuple-element.124, ...), kind=kLoop, calls=%fused_computation.31 | loop fusion | flops 22020096 | bytes 31475712 | tf_op jit(solution)/shard_map/while/body/eval_jaxpr/convert_element_type | solution.py:91
  638.8 9.7 %convert_bitcast_fusion = bf16[2048,1,2048]{2,0,1:T(8,128)(2,1)} fusion(bf16[2048,384]{0,1:T(8,128)(2,1)} %bitcast.239, bf16[2048,384]{0,1:T(8,128)(2,1)} %bitcast.240), kind=kOutput, calls=%fused_computation.17 | convolution fusion | flops 3225419776 | bytes 11534336 | tf_op jit(solution)/shard_map/rsc,dc->rsd/dot_general | solution.py:272
  651.9 8.9 %fusion.27 = f32[512,2048]{1,0:T(8,128)S(1)} fusion(bf16[2048,1,2048]{2,0,1:T(8,128)(2,1)} %all-gather.6.cloned.1.call-done, f32[]{:T(128)S(6)} %div.167, f32[2048,512]{1,0:T(8,128)} %copy-done.100, f32[512]{0:T(512)S(1)} %copy-done.99), kind=kOutput, calls=%fused_computation.60 | convolution fusion | flops 4306501632 | bytes 16779268 | tf_op jit(solution)/shard_map/rsf,rsd->fd/dot_general | solution.py:216
  672.6 7.2 fusion.30
  686.7 10.6 %collective-permute-done.31 = bf16[512,4,256]{2,0,1:T(8,128)(2,1)} collective-permute-done((bf16[512,4,256]{2,0,1:T(8,128)(2,1)}, bf16[512,4,256]{2,0,1:T(8,128)(2,1)}, u32[]{:S(2)}, u32[]{:S(2)}) %collective-permute-start.31) | collective-permute-done | bytes 1048608 | tf_op jit(solution)/shard_map/ppermute | solution.py:364
  699.5 9.2 %collective-permute-done.28 = bf16[4,256,512]{2,1,0:T(8,128)(2,1)} collective-permute-done((bf16[4,256,512]{2,1,0:T(8,128)(2,1)}, bf16[4,256,512]{2,1,0:T(8,128)(2,1)}, u32[]{:S(2)}, u32[]{:S(2)}) %collective-permute-start.28) | collective-permute-done | bytes 1048608 | tf_op jit(solution)/shard_map/ppermute | solution.py:364
  739.2 7.0 fusion.36
  762.4 29.7 %collective-permute-done.22 = bf16[4,256,3,1,128]{4,3,2,1,0:T(2,128)(2,1)} collective-permute-done((bf16[4,256,3,1,128]{4,3,2,1,0:T(2,128)(2,1)S(1)}, bf16[4,256,3,1,128]{4,3,2,1,0:T(2,128)(2,1)}, u32[]{:S(2)}, u32[]{:S(2)}) %collective-permute-start.22) | collective-permute-done | bytes 786464 | tf_op jit(solution)/shard_map/ppermute | solution.py:364
  810.1 5.7 collective-permute-done.24
  (441 shorter events, 250.9 us)
Async XLA Ops:
  7.2 78.3 %all-gather.4.cloned.1.call-start = ((), (), s32[]{:S(2)}) async-start(), calls=%async_computation.4 | async-start | bytes 8912896 | tf_op jit(solution)/shard_map/all_gather | solution.py:154
  12.2 146.3 %all-gather.6.cloned.1.call-start = ((), (), s32[]{:S(2)}) async-start(), calls=%async_computation.5 | async-start | bytes 8912896 | tf_op jit(solution)/shard_map/all_gather | solution.py:189
  16.8 229.8 %reduce-scatter.5.cloned.1.call-start = ((), (), s32[]{:S(2)}) async-start(), calls=%async_computation.6 | async-start | bytes 8912896 | tf_op jit(solution)/shard_map/reduce_scatter | solution.py:195
  158.6 163.3 %all-gather.8.cloned.1.call-start = ((), (), s32[]{:S(2)}) async-start(), calls=%async_computation.7 | async-start | bytes 8912896 | tf_op jit(solution)/shard_map/all_gather | solution.py:202
  251.6 183.9 %reduce-scatter.7.cloned.1.call-start = ((), (), s32[]{:S(2)}) async-start(), calls=%async_computation.8 | async-start | bytes 8912896 | tf_op jit(solution)/shard_map/reduce_scatter | solution.py:231
  351.0 406.9 %reduce-scatter.11.cloned.1.call-start = ((), (), s32[]{:S(2)}) async-start(), calls=%async_computation.10 | async-start | bytes 8912896 | tf_op jit(solution)/shard_map/reduce_scatter | solution.py:271
  440.6 15.8 %collective-permute-start = (bf16[128,1,2048]{2,0,1:T(8,128)(2,1)S(1)}, bf16[128,1,2048]{2,0,1:T(8,128)(2,1)S(1)}, u32[]{:S(2)}, u32[]{:S(2)}) collective-permute-start(bf16[128,1,2048]{2,0,1:T(8,128)(2,1)S(1)} %get-tuple-element.89), channel_id=1, source_target_pairs={{0,1},{1,2},{2,3},{3,4},{4,5},{5,6},{6,7},{7,8},{8,9},{9,10},{10,1... | collective-permute-start | bytes 1572872 | tf_op jit(solution)/shard_map/ppermute | solution.py:25
  456.4 14.8 %collective-permute-start.1 = (bf16[128,1,2048]{2,0,1:T(8,128)(2,1)S(1)}, bf16[128,1,2048]{2,0,1:T(8,128)(2,1)S(1)}, u32[]{:S(2)}, u32[]{:S(2)}) collective-permute-start(bf16[128,1,2048]{2,0,1:T(8,128)(2,1)S(1)} %collective-permute-done), channel_id=1, source_target_pairs={{0,1},{1,2},{2,3},{3,4},{4,5},{5,6},{6,7},{7,8},{8,9},{9,10},{10,1... | collective-permute-start | bytes 1572872 | tf_op jit(solution)/shard_map/ppermute | solution.py:25
  456.4 14.8 %collective-permute-start.8 = (bf16[128,1,2048]{2,0,1:T(8,128)(2,1)S(1)}, bf16[128,1,2048]{2,0,1:T(8,128)(2,1)}, u32[]{:S(2)}, u32[]{:S(2)}) collective-permute-start(bf16[128,1,2048]{2,0,1:T(8,128)(2,1)S(1)} %get-tuple-element.89), channel_id=1, source_target_pairs={{1,0},{2,1},{3,2},{4,3},{5,4},{6,5},{7,6},{8,7},{9,8},{10,9},{11,1... | collective-permute-start | bytes 1572872 | tf_op jit(solution)/shard_map/ppermute | solution.py:27
  471.2 14.0 %collective-permute-start.2 = (bf16[128,1,2048]{2,0,1:T(8,128)(2,1)S(1)}, bf16[128,1,2048]{2,0,1:T(8,128)(2,1)}, u32[]{:S(2)}, u32[]{:S(2)}) collective-permute-start(bf16[128,1,2048]{2,0,1:T(8,128)(2,1)S(1)} %collective-permute-done.1), channel_id=1, source_target_pairs={{0,1},{1,2},{2,3},{3,4},{4,5},{5,6},{6,7},{7,8},{8,9},{9,10},{10,1... | collective-permute-start | bytes 1572872 | tf_op jit(solution)/shard_map/ppermute | solution.py:25
  471.2 14.0 %collective-permute-start.9 = (bf16[128,1,2048]{2,0,1:T(8,128)(2,1)}, bf16[128,1,2048]{2,0,1:T(8,128)(2,1)}, u32[]{:S(2)}, u32[]{:S(2)}) collective-permute-start(bf16[128,1,2048]{2,0,1:T(8,128)(2,1)} %collective-permute-done.8), channel_id=1, source_target_pairs={{1,0},{2,1},{3,2},{4,3},{5,4},{6,5},{7,6},{8,7},{9,8},{10,9},{11,1... | collective-permute-start | bytes 1572872 | tf_op jit(solution)/shard_map/ppermute | solution.py:27
  485.2 13.3 %collective-permute-start.3 = (bf16[128,1,2048]{2,0,1:T(8,128)(2,1)}, bf16[128,1,2048]{2,0,1:T(8,128)(2,1)}, u32[]{:S(2)}, u32[]{:S(2)}) collective-permute-start(bf16[128,1,2048]{2,0,1:T(8,128)(2,1)} %collective-permute-done.2), channel_id=1, source_target_pairs={{0,1},{1,2},{2,3},{3,4},{4,5},{5,6},{6,7},{7,8},{8,9},{9,10},{10,1... | collective-permute-start | bytes 1572872 | tf_op jit(solution)/shard_map/ppermute | solution.py:25
  485.3 17.0 %collective-permute-start.10 = (bf16[128,1,2048]{2,0,1:T(8,128)(2,1)}, bf16[128,1,2048]{2,0,1:T(8,128)(2,1)S(1)}, u32[]{:S(2)}, u32[]{:S(2)}) collective-permute-start(bf16[128,1,2048]{2,0,1:T(8,128)(2,1)} %collective-permute-done.9), channel_id=1, source_target_pairs={{1,0},{2,1},{3,2},{4,3},{5,4},{6,5},{7,6},{8,7},{9,8},{10,9},{11,1... | collective-permute-start | bytes 1572872 | tf_op jit(solution)/shard_map/ppermute | solution.py:27
  498.5 13.0 %collective-permute-start.4 = (bf16[128,1,2048]{2,0,1:T(8,128)(2,1)}, bf16[128,1,2048]{2,0,1:T(8,128)(2,1)S(1)}, u32[]{:S(2)}, u32[]{:S(2)}) collective-permute-start(bf16[128,1,2048]{2,0,1:T(8,128)(2,1)} %collective-permute-done.3), channel_id=1, source_target_pairs={{0,1},{1,2},{2,3},{3,4},{4,5},{5,6},{6,7},{7,8},{8,9},{9,10},{10,1... | collective-permute-start | bytes 1572872 | tf_op jit(solution)/shard_map/ppermute | solution.py:25
  502.3 12.1 %collective-permute-start.11 = (bf16[128,1,2048]{2,0,1:T(8,128)(2,1)S(1)}, bf16[128,1,2048]{2,0,1:T(8,128)(2,1)S(1)}, u32[]{:S(2)}, u32[]{:S(2)}) collective-permute-start(bf16[128,1,2048]{2,0,1:T(8,128)(2,1)S(1)} %collective-permute-done.10), channel_id=1, source_target_pairs={{1,0},{2,1},{3,2},{4,3},{5,4},{6,5},{7,6},{8,7},{9,8},{10,9},{11,1... | collective-permute-start | bytes 1572872 | tf_op jit(solution)/shard_map/ppermute | solution.py:27
  511.5 13.9 %collective-permute-start.5 = (bf16[128,1,2048]{2,0,1:T(8,128)(2,1)S(1)}, bf16[128,1,2048]{2,0,1:T(8,128)(2,1)S(1)}, u32[]{:S(2)}, u32[]{:S(2)}) collective-permute-start(bf16[128,1,2048]{2,0,1:T(8,128)(2,1)S(1)} %collective-permute-done.4), channel_id=1, source_target_pairs={{0,1},{1,2},{2,3},{3,4},{4,5},{5,6},{6,7},{7,8},{8,9},{9,10},{10,1... | collective-permute-start | bytes 1572872 | tf_op jit(solution)/shard_map/ppermute | solution.py:25
  515.2 13.9 %collective-permute-start.12 = (bf16[128,1,2048]{2,0,1:T(8,128)(2,1)S(1)}, bf16[128,1,2048]{2,0,1:T(8,128)(2,1)}, u32[]{:S(2)}, u32[]{:S(2)}) collective-permute-start(bf16[128,1,2048]{2,0,1:T(8,128)(2,1)S(1)} %collective-permute-done.11), channel_id=1, source_target_pairs={{1,0},{2,1},{3,2},{4,3},{5,4},{6,5},{7,6},{8,7},{9,8},{10,9},{11,1... | collective-permute-start | bytes 1572872 | tf_op jit(solution)/shard_map/ppermute | solution.py:27
  525.3 14.7 %collective-permute-start.6 = (bf16[128,1,2048]{2,0,1:T(8,128)(2,1)S(1)}, bf16[128,1,2048]{2,0,1:T(8,128)(2,1)}, u32[]{:S(2)}, u32[]{:S(2)}) collective-permute-start(bf16[128,1,2048]{2,0,1:T(8,128)(2,1)S(1)} %collective-permute-done.5), channel_id=1, source_target_pairs={{0,1},{1,2},{2,3},{3,4},{4,5},{5,6},{6,7},{7,8},{8,9},{9,10},{10,1... | collective-permute-start | bytes 1572872 | tf_op jit(solution)/shard_map/ppermute | solution.py:25
  529.1 18.2 %collective-permute-start.13 = (bf16[128,1,2048]{2,0,1:T(8,128)(2,1)}, bf16[128,1,2048]{2,0,1:T(8,128)(2,1)}, u32[]{:S(2)}, u32[]{:S(2)}) collective-permute-start(bf16[128,1,2048]{2,0,1:T(8,128)(2,1)} %collective-permute-done.12), channel_id=1, source_target_pairs={{1,0},{2,1},{3,2},{4,3},{5,4},{6,5},{7,6},{8,7},{9,8},{10,9},{11,1... | collective-permute-start | bytes 1572872 | tf_op jit(solution)/shard_map/ppermute | solution.py:27
  540.1 12.8 %collective-permute-start.7 = (bf16[128,1,2048]{2,0,1:T(8,128)(2,1)}, bf16[128,1,2048]{2,0,1:T(8,128)(2,1)}, u32[]{:S(2)}, u32[]{:S(2)}) collective-permute-start(bf16[128,1,2048]{2,0,1:T(8,128)(2,1)} %collective-permute-done.6), channel_id=1, source_target_pairs={{0,1},{1,2},{2,3},{3,4},{4,5},{5,6},{6,7},{7,8},{8,9},{9,10},{10,1... | collective-permute-start | bytes 1572872 | tf_op jit(solution)/shard_map/ppermute | solution.py:25
  547.3 28.9 %collective-permute-start.14 = (bf16[128,1,2048]{2,0,1:T(8,128)(2,1)}, bf16[128,1,2048]{2,0,1:T(8,128)(2,1)S(1)}, u32[]{:S(2)}, u32[]{:S(2)}) collective-permute-start(bf16[128,1,2048]{2,0,1:T(8,128)(2,1)} %collective-permute-done.13), channel_id=1, source_target_pairs={{1,0},{2,1},{3,2},{4,3},{5,4},{6,5},{7,6},{8,7},{9,8},{10,9},{11,1... | collective-permute-start | bytes 1572872 | tf_op jit(solution)/shard_map/ppermute | solution.py:27
  648.5 170.8 %reduce-scatter.9.cloned.1.call-start = ((), (), s32[]{:S(2)}) async-start(), calls=%async_computation.9 | async-start | bytes 8912896 | tf_op jit(solution)/shard_map/reduce_scatter | solution.py:248
  670.9 26.4 %collective-permute-start.31 = (bf16[512,4,256]{2,0,1:T(8,128)(2,1)}, bf16[512,4,256]{2,0,1:T(8,128)(2,1)}, u32[]{:S(2)}, u32[]{:S(2)}) collective-permute-start(bf16[512,4,256]{2,0,1:T(8,128)(2,1)} %select_convert_fusion), channel_id=1, source_target_pairs={{0,64},{32,96},{64,0},{96,32},{1,65},{33,97},{65,1},{97,33},{2,66}... | collective-permute-start | bytes 3145736 | tf_op jit(solution)/shard_map/ppermute | solution.py:364
  682.2 26.6 %collective-permute-start.28 = (bf16[4,256,512]{2,1,0:T(8,128)(2,1)}, bf16[4,256,512]{2,1,0:T(8,128)(2,1)}, u32[]{:S(2)}, u32[]{:S(2)}) collective-permute-start(bf16[4,256,512]{2,1,0:T(8,128)(2,1)} %bitcast.76), channel_id=1, source_target_pairs={{0,64},{32,96},{64,0},{96,32},{1,65},{33,97},{65,1},{97,33},{2,66}... | collective-permute-start | bytes 3145736 | tf_op jit(solution)/shard_map/ppermute | solution.py:364
  699.4 11.2 %collective-permute-start.32 = (bf16[512,2,256]{2,0,1:T(8,128)(2,1)S(1)}, bf16[512,2,256]{2,0,1:T(8,128)(2,1)S(1)}, u32[]{:S(2)}, u32[]{:S(2)}) collective-permute-start(bf16[512,2,256]{2,0,1:T(8,128)(2,1)S(1)} %select_convert_fusion.3), channel_id=1, source_target_pairs={{0,32},{32,0},{64,96},{96,64},{1,33},{33,1},{65,97},{97,65},{2,34}... | collective-permute-start | bytes 1572872 | tf_op jit(solution)/shard_map/ppermute | solution.py:364
  711.6 11.0 %collective-permute-start.33 = (bf16[512,1,256]{2,0,1:T(8,128)(2,1)}, bf16[512,1,256]{2,0,1:T(8,128)(2,1)S(1)}, u32[]{:S(2)}, u32[]{:S(2)}) collective-permute-start(bf16[512,1,256]{2,0,1:T(8,128)(2,1)} %select_convert_fusion.5), channel_id=1, source_target_pairs={{0,16},{16,0},{1,17},{17,1},{2,18},{18,2},{3,19},{19,3},{4,20},{20... | collective-permute-start | bytes 786440 | tf_op jit(solution)/shard_map/ppermute | solution.py:364
  716.5 11.4 %collective-permute-start.30 = (bf16[1,256,512]{2,1,0:T(8,128)(2,1)S(1)}, bf16[1,256,512]{2,1,0:T(8,128)(2,1)S(1)}, u32[]{:S(2)}, u32[]{:S(2)}) collective-permute-start(bf16[1,256,512]{2,1,0:T(8,128)(2,1)S(1)} %select_convert_fusion.6), channel_id=1, source_target_pairs={{0,16},{16,0},{1,17},{17,1},{2,18},{18,2},{3,19},{19,3},{4,20},{20... | collective-permute-start | bytes 786440 | tf_op jit(solution)/shard_map/ppermute | solution.py:364
  737.6 10.1 %collective-permute-start.25 = (bf16[1,128,4,256]{3,1,2,0:T(8,128)(2,1)S(1)}, bf16[1,128,4,256]{3,1,2,0:T(8,128)(2,1)S(1)}, u32[]{:S(2)}, u32[]{:S(2)}) collective-permute-start(bf16[1,128,4,256]{3,1,2,0:T(8,128)(2,1)S(1)} %select_convert_fusion.7), channel_id=1, source_target_pairs={{0,64},{32,96},{64,0},{96,32},{1,65},{33,97},{65,1},{97,33},{2,66}... | collective-permute-start | bytes 786440 | tf_op jit(solution)/shard_map/ppermute | solution.py:364
  755.7 36.4 %collective-permute-start.22 = (bf16[4,256,3,1,128]{4,3,2,1,0:T(2,128)(2,1)S(1)}, bf16[4,256,3,1,128]{4,3,2,1,0:T(2,128)(2,1)}, u32[]{:S(2)}, u32[]{:S(2)}) collective-permute-start(bf16[4,256,3,1,128]{4,3,2,1,0:T(2,128)(2,1)S(1)} %copy.55), channel_id=1, source_target_pairs={{0,64},{32,96},{64,0},{96,32},{1,65},{33,97},{65,1},{97,33},{2,66}... | collective-permute-start | bytes 2359304 | tf_op jit(solution)/shard_map/ppermute | solution.py:364
  762.3 34.1 %collective-permute-start.15 = (f32[8,8,192]{2,0,1:T(8,128)S(1)}, f32[8,8,192]{2,0,1:T(8,128)S(1)}, u32[]{:S(2)}, u32[]{:S(2)}) collective-permute-start(f32[8,8,192]{2,0,1:T(8,128)S(1)} %slice_select_fusion.2), channel_id=1, source_target_pairs={{0,8},{1,9},{2,10},{3,11},{4,12},{5,13},{6,14},{7,15},{8,0},{9,1},... | collective-permute-start | bytes 147464 | tf_op jit(solution)/shard_map/ppermute | solution.py:364
  806.4 9.4 %collective-permute-start.24 = (bf16[1,256,3,1,128]{4,3,2,1,0:T(2,128)(2,1)S(1)}, bf16[1,256,3,1,128]{4,3,2,1,0:T(2,128)(2,1)S(1)}, u32[]{:S(2)}, u32[]{:S(2)}) collective-permute-start(bf16[1,256,3,1,128]{4,3,2,1,0:T(2,128)(2,1)S(1)} %fusion.96), channel_id=1, source_target_pairs={{0,16},{16,0},{1,17},{17,1},{2,18},{18,2},{3,19},{19,3},{4,20},{20... | collective-permute-start | bytes 589832 | tf_op jit(solution)/shard_map/ppermute | solution.py:364
  809.7 7.5 collective-permute-start.19
  (113 other events, 2519.4 us)
Sparse Core Ops, SparseCore 0:
  12.4 73.0 all-gather.3
  88.2 70.3 all-gather.5
  162.0 84.6 reduce-scatter.4
  251.8 70.0 all-gather.7
  351.1 84.4 reduce-scatter.6
  648.7 81.5 reduce-scatter.10
  733.6 84.6 reduce-scatter.8
